TPU v7x, 256 devices: a whole 4x4x8 slice. The times are simulated.
256 devices in a mesh: tm: 16 (over y, x_hi, core), space: 16 (over x_lo, z).
Axes of the slice: x: 4 (x_hi: 2, x_lo: 2; x = x_hi * 2 + x_lo), y: 4, z: 8, core: 2. Of those that a mesh axis runs over, the one named last changes fastest.
Arguments:
- query: bfloat16 [16, 2048, 1536], P('tm', 'space')
- key_new: bfloat16 [16, 2048, 1536], P('tm', 'space')
- value_new: bfloat16 [16, 2048, 1536], P('tm', 'space'), may hold values from -6 to 6
- key_clean: bfloat16 [16, 2048, 1536], P('tm', 'space'), may hold values from -6 to 6
- value_clean: bfloat16 [16, 2048, 1536], P('tm', 'space'), may hold values from -6 to 6
- out_weight: bfloat16 [1536, 1536], replicated, may hold values from -1.25 to 1.25
- step_gate: float32 [4, 1536], replicated, may hold values from 0.5 to 1.5
- noise_step: int32 [16], P('tm'), may hold values from 0 to 3
- tile_mask: int32 [16, 16, 3], P('tm', 'space'), may hold values 0 or 1
Outputs:
- gated_out: bfloat16 [16, 2048, 1536], P('tm', 'space')
All inputs are finite; a program needn't handle non-finite values. No bound on the sum of `tile_mask` on one device may be relied on, other than what follows from the above.
Results may differ from a plain program's by a relative error of at most 0.0075.
Values may be sent and summed in bfloat16 or wider, within the bound.
No kernel may reach another device: no remote copies, remote signals or barrier semaphores. Data moves between devices by JAX's collectives and lax.ppermute only.
A program may use at most 64 MiB of HBM per device.

v0:
```python
import functools
import math

import jax
import jax.numpy as jnp
from jax import lax
from jax.experimental import pallas as pl
from jax.experimental.pallas import tpu as pltpu
from jax.sharding import PartitionSpec as P


HEADS = 12
HEAD = 128
TILE = 128
D = HEADS * HEAD
LOG2E = 1.4426950408889634
NEG = -1e30

PARAMS = pltpu.CompilerParams(vmem_limit_bytes=24 * 2**20)


def past_bias(group):
    even = lax.rem(group, 2) == 0
    ok_two = group >= 2
    ok_side = jnp.where(even, group >= 4, group >= 1)
    ok_swap = jnp.where(even, group >= 2, group >= 3)
    return [jnp.where(ok, 0.0, NEG).astype(jnp.float32) for ok in (ok_two, ok_side, ok_swap)]


def head_partial(q, keys, values, biases):
    scale = LOG2E / math.sqrt(HEAD)
    scores = []
    for key, bias in zip(keys, biases):
        s = lax.dot_general(q, key, (((1,), (1,)), ((), ())), preferred_element_type=jnp.float32)
        s = s * scale
        scores.append(s if bias is None else s + bias)
    peak = functools.reduce(jnp.maximum, scores)
    peak = jnp.max(peak, axis=-1, keepdims=True)
    weights = [jnp.exp2(s - peak) for s in scores]
    total = jnp.sum(functools.reduce(jnp.add, weights), axis=-1, keepdims=True)
    w = jnp.concatenate([x.astype(jnp.bfloat16) for x in weights], axis=1)
    v = jnp.concatenate(values, axis=0)
    accum = jnp.dot(w, v, preferred_element_type=jnp.float32)
    return accum * (1.0 / total), peak + jnp.log2(total)


def chunk_blocks(h, blocks):
    cols = slice(h * HEAD, (h + 1) * HEAD)
    return cols, [r[0, :, cols] for r in blocks[0::2]], [r[0, :, cols] for r in blocks[1::2]]


def stage_kernel(tiles_all, step, mask, gate, q, kn, vn, q_out, kn_out, vn_out, gate_out, bias_out, sems):
    copies = [
        pltpu.make_async_copy(source, target, sems.at[i])
        for i, (source, target) in enumerate(((q, q_out), (kn, kn_out), (vn, vn_out)))
    ]
    for copy in copies:
        copy.start()
    gate_out[...] = gate[pl.ds(step[0], 1), :]
    tile = lax.axis_index("space")
    even = lax.rem(tile, 2) == 0
    use_low = (mask[0, 0, 0] == 1) & (tile > 0)
    use_high = (mask[0, 0, 2] == 1) & (tile < tiles_all - 1)
    zero = jnp.zeros((1, HEAD), jnp.float32)
    low = jnp.where(use_low, zero, NEG)
    high = jnp.where(use_high, zero, NEG)
    bias_out[0:1, :] = jnp.where(even, high, low)
    bias_out[1:2, :] = jnp.where(even, low, high)
    for copy in copies:
        copy.wait()


def neighbour_kernel(first, heads, q_one, q_two, *refs):
    blocks, (to_one, to_two) = refs[:8], refs[8:]
    biases = [None] + past_bias(lax.axis_index("tm"))
    lane = lax.broadcasted_iota(jnp.int32, (2 * TILE, HEAD), 1)
    stats = jnp.zeros((2 * TILE, HEAD), jnp.float32)
    width = heads * HEAD
    for h in range(heads):
        cols, keys, values = chunk_blocks(first + h, blocks)
        q = jnp.concatenate([q_one[0, :, cols], q_two[0, :, cols]], axis=0)
        part, lse = head_partial(q, keys, values, biases)
        part = part.astype(jnp.bfloat16)
        here = slice(h * HEAD, (h + 1) * HEAD)
        to_one[:, here] = part[:TILE]
        to_two[:, here] = part[TILE:]
        stats = jnp.where(lane == h, lse, stats)
    first_part = stats.astype(jnp.bfloat16).astype(jnp.float32)
    rest = stats - first_part
    second_part = rest.astype(jnp.bfloat16).astype(jnp.float32)
    third_part = rest - second_part
    packed = first_part + pltpu.roll(second_part, 16, 1) + pltpu.roll(third_part, 32, 1)
    packed = packed.astype(jnp.bfloat16)
    to_one[:, width:] = packed[:TILE]
    to_two[:, width:] = packed[TILE:]


def own_kernel(first, heads, q, *refs):
    blocks, (out, out_lse) = refs[:8], refs[8:]
    biases = [None] + past_bias(lax.axis_index("tm"))
    lane = lax.broadcasted_iota(jnp.int32, (TILE, HEAD), 1)
    stats = jnp.zeros((TILE, HEAD), jnp.float32)
    for h in range(heads):
        cols, keys, values = chunk_blocks(first + h, blocks)
        part, lse = head_partial(q[0, :, cols], keys, values, biases)
        out[:, h * HEAD : (h + 1) * HEAD] = part
        stats = jnp.where(lane == h, lse, stats)
    out_lse[...] = stats


def unpacked(block):
    packed = block.astype(jnp.float32)
    return packed + pltpu.roll(packed, HEAD - 16, 1) + pltpu.roll(packed, HEAD - 32, 1)


def merge_kernel(first, heads, has_sum, last, bias, own, own_lse, one, two, weight, *rest):
    rest = list(rest)
    gate = rest.pop(0) if last else None
    before = rest.pop(0) if has_sum else None
    out, attended = rest
    width = heads * HEAD
    lse_own = own_lse[...]
    lse_one = unpacked(one[:, width:]) + bias[0:1, :]
    lse_two = unpacked(two[:, width:]) + bias[1:2, :]
    peak = jnp.maximum(jnp.maximum(lse_own, lse_one), lse_two)
    w_own = jnp.exp2(lse_own - peak)
    w_one = jnp.exp2(lse_one - peak)
    w_two = jnp.exp2(lse_two - peak)
    inv = 1.0 / (w_own + w_one + w_two)
    w_own, w_one, w_two = w_own * inv, w_one * inv, w_two * inv
    for h in range(heads):
        cols = slice(h * HEAD, (h + 1) * HEAD)
        lane = slice(h, h + 1)
        mixed = (
            w_own[:, lane] * own[:, cols]
            + w_one[:, lane] * one[:, cols].astype(jnp.float32)
            + w_two[:, lane] * two[:, cols].astype(jnp.float32)
        )
        attended[:, cols] = mixed.astype(jnp.bfloat16)
    att = attended[...]
    rows = slice(first * HEAD, first * HEAD + width)
    for n in range(0, D, 256):
        cols = slice(n, n + 256)
        projected = jnp.dot(att, weight[rows, cols], preferred_element_type=jnp.float32)
        if has_sum:
            projected = projected + before[:, cols]
        if last:
            out[0, :, cols] = (gate[:, cols] * projected).astype(jnp.bfloat16)
        else:
            out[:, cols] = projected


VMEM = pl.BlockSpec(memory_space=pltpu.VMEM)
SMEM = pl.BlockSpec(memory_space=pltpu.SMEM)
HBM = pl.BlockSpec(memory_space=pltpu.HBM)
CHUNKS = ((0, 8), (8, 4))


def cost(flops, moved, exps=0):
    return pl.CostEstimate(flops=flops, bytes_accessed=moved, transcendentals=exps)


def stage(space_size, noise_step, tile_mask, step_gate, query, key_new, value_new):
    block = jax.ShapeDtypeStruct((1, TILE, D), jnp.bfloat16)
    return pl.pallas_call(
        functools.partial(stage_kernel, space_size),
        out_shape=(
            block,
            block,
            block,
            jax.ShapeDtypeStruct((1, D), jnp.float32),
            jax.ShapeDtypeStruct((8, HEAD), jnp.float32),
        ),
        in_specs=[SMEM, SMEM, VMEM, HBM, HBM, HBM],
        out_specs=(VMEM,) * 5,
        scratch_shapes=[pltpu.SemaphoreType.DMA((3,))],
        cost_estimate=cost(0, 12 * TILE * D),
        compiler_params=PARAMS,
        name="stage",
    )(noise_step, tile_mask, step_gate, *in_hbm(query, key_new, value_new))


def neighbour(first, heads, *args):
    width = heads * HEAD
    return pl.pallas_call(
        functools.partial(neighbour_kernel, first, heads),
        out_shape=(jax.ShapeDtypeStruct((TILE, width + HEAD), jnp.bfloat16),) * 2,
        in_specs=[VMEM] * 10,
        out_specs=(VMEM, VMEM),
        cost_estimate=cost(4 * 256 * 512 * width, 24 * TILE * width, heads * 256 * 512),
        compiler_params=PARAMS,
    )(*args)


def own(first, heads, *args):
    width = heads * HEAD
    return pl.pallas_call(
        functools.partial(own_kernel, first, heads),
        out_shape=(
            jax.ShapeDtypeStruct((TILE, width), jnp.float32),
            jax.ShapeDtypeStruct((TILE, HEAD), jnp.float32),
        ),
        in_specs=[VMEM] * 9,
        out_specs=(VMEM, VMEM),
        cost_estimate=cost(4 * 128 * 512 * width, 22 * TILE * width, heads * 128 * 512),
        compiler_params=PARAMS,
    )(*args)


def merge(first, heads, has_sum, last, *args):
    width = heads * HEAD
    if last:
        result = jax.ShapeDtypeStruct((1, TILE, D), jnp.bfloat16)
    else:
        result = jax.ShapeDtypeStruct((TILE, D), jnp.float32)
    return pl.pallas_call(
        functools.partial(merge_kernel, first, heads, has_sum, last),
        out_shape=result,
        in_specs=[VMEM] * len(args),
        out_specs=VMEM,
        scratch_shapes=[pltpu.VMEM((TILE, width), jnp.bfloat16)],
        cost_estimate=cost(2 * TILE * D * width, 2 * D * width + 8 * TILE * D),
        compiler_params=PARAMS,
    )(*args)


def in_hbm(*arrays):
    return [pltpu.with_memory_space_constraint(a, pltpu.HBM) for a in arrays]


def on_device(
    tm_size,
    space_size,
    query,
    key_new,
    value_new,
    key_clean,
    value_clean,
    out_weight,
    step_gate,
    noise_step,
    tile_mask,
):
    two_back = [(t, (t + 2) % tm_size) for t in range(tm_size)]
    side = [(t, (t + (1 if t % 2 == 0 else 3)) % tm_size) for t in range(tm_size)]
    swap = [(t, t + 1 if t % 2 == 0 else t - 1) for t in range(tm_size)]

    one = [(s, s + 1 if s % 2 == 0 else s - 1) for s in range(space_size)]
    two = []
    for t in range(tm_size):
        for s in range(space_size):
            to = s - 1 if s % 2 == 0 else s + 1
            inside = 0 <= to < space_size
            target = (t, to) if inside else (swap[t][1], s)
            two.append((t * space_size + s, target[0] * space_size + target[1]))
    both = ("tm", "space")

    k2 = lax.ppermute(key_clean, "tm", two_back)
    v2 = lax.ppermute(value_clean, "tm", two_back)
    ks = lax.ppermute(key_clean, "tm", side)
    vs = lax.ppermute(value_clean, "tm", side)
    q_one = lax.ppermute(query, "space", one)
    q_two = lax.ppermute(query, both, two)
    kx = lax.ppermute(k2, "tm", swap)
    vx = lax.ppermute(v2, "tm", swap)
    q, kn, vn, gate_row, bias = stage(
        space_size, noise_step, tile_mask, step_gate, query, key_new, value_new
    )
    blocks = (kn, vn, k2, v2, ks, vs, kx, vx)
    total = None
    for i, (first, heads) in enumerate(CHUNKS):
        to_one, to_two = neighbour(first, heads, q_one, q_two, *blocks)
        from_one = lax.ppermute(to_one, "space", one)
        from_two = lax.ppermute(to_two, both, two)
        mine, mine_lse = own(first, heads, q, *blocks)
        last = i == len(CHUNKS) - 1
        args = [bias, mine, mine_lse, from_one, from_two, out_weight]
        args += [gate_row] if last else []
        args += [total] if i > 0 else []
        total = merge(first, heads, i > 0, last, *args)
    return total


def solution(mesh):
    placed = (
        P("tm", "space", None),
        P("tm", "space", None),
        P("tm", "space", None),
        P("tm", "space", None),
        P("tm", "space", None),
        P(),
        P(),
        P("tm"),
        P("tm", "space", None),
    )
    body = functools.partial(on_device, mesh.shape["tm"], mesh.shape["space"])
    return jax.shard_map(
        body, mesh=mesh, in_specs=placed, out_specs=P("tm", "space", None), check_vma=False
    )
```

profile of v0, /device:TPU:194, one launch (start us, length us, event | category | flops | bytes accessed | tf_op | source)
XLA Modules:
  0.0 53.7 jit_solution(4117144993874710291)
XLA Ops:
  0.0 2.1 %collective-permute-start = (bf16[1,128,1536]{2,1,0:T(8,128)(2,1)}, bf16[1,128,1536]{2,1,0:T(8,128)(2,1)S(1)}, u32[]{:S(2)}, u32[]{:S(2)}) collective-permute-start(bf16[1,128,1536]{2,1,0:T(8,128)(2,1)} %param.12), channel_id=1, source_target_pairs={{0,32},{16,48},{32,64},{48,80},{64,96},{80,112},{96,128},{112,144}... | collective-permute-start | bytes 1179656 | tf_op jit(solution)/shard_map/ppermute | solution.py:258
  2.1 2.4 %collective-permute-start.1 = (bf16[1,128,1536]{2,1,0:T(8,128)(2,1)}, bf16[1,128,1536]{2,1,0:T(8,128)(2,1)S(1)}, u32[]{:S(2)}, u32[]{:S(2)}) collective-permute-start(bf16[1,128,1536]{2,1,0:T(8,128)(2,1)} %param.13), channel_id=1, source_target_pairs={{0,32},{16,48},{32,64},{48,80},{64,96},{80,112},{96,128},{112,144}... | collective-permute-start | bytes 1179656 | tf_op jit(solution)/shard_map/ppermute | solution.py:259
  4.5 0.0 collective-permute-start.2
  4.5 1.7 %collective-permute-start.3 = (bf16[1,128,1536]{2,1,0:T(8,128)(2,1)}, bf16[1,128,1536]{2,1,0:T(8,128)(2,1)S(1)}, u32[]{:S(2)}, u32[]{:S(2)}) collective-permute-start(bf16[1,128,1536]{2,1,0:T(8,128)(2,1)} %param.13), channel_id=1, source_target_pairs={{0,16},{16,64},{32,48},{48,96},{64,80},{80,128},{96,112},{112,160}... | collective-permute-start | bytes 1179656 | tf_op jit(solution)/shard_map/ppermute | solution.py:261
  6.2 1.0 %collective-permute-start.6 = (bf16[1,128,1536]{2,1,0:T(8,128)(2,1)}, bf16[1,128,1536]{2,1,0:T(8,128)(2,1)S(1)}, u32[]{:S(2)}, u32[]{:S(2)}) collective-permute-start(bf16[1,128,1536]{2,1,0:T(8,128)(2,1)} %q.1), channel_id=1, source_target_pairs={{0,1},{1,0},{2,3},{3,2},{4,5},{5,4},{6,7},{7,6},{8,9},{9,8},{10,11... | collective-permute-start | bytes 1179656 | tf_op jit(solution)/shard_map/ppermute | solution.py:262
  7.3 8.7 %collective-permute-done.refs_2_ = bf16[1,128,1536]{2,1,0:T(8,128)(2,1)S(1)} collective-permute-done((bf16[1,128,1536]{2,1,0:T(8,128)(2,1)}, bf16[1,128,1536]{2,1,0:T(8,128)(2,1)S(1)}, u32[]{:S(2)}, u32[]{:S(2)}) %collective-permute-start) | collective-permute-done | bytes 393248 | tf_op jit(solution)/shard_map/ppermute | solution.py:258
  15.9 1.0 %collective-permute-start.7 = (bf16[1,128,1536]{2,1,0:T(8,128)(2,1)}, bf16[1,128,1536]{2,1,0:T(8,128)(2,1)S(1)}, u32[]{:S(2)}, u32[]{:S(2)}) collective-permute-start(bf16[1,128,1536]{2,1,0:T(8,128)(2,1)} %q.1), channel_id=1, source_target_pairs={{0,16},{1,2},{2,1},{3,4},{4,3},{5,6},{6,5},{7,8},{8,7},{9,10},{10,... | collective-permute-start | bytes 1179656 | tf_op jit(solution)/shard_map/ppermute | solution.py:263
  16.9 6.3 %collective-permute-done.1.refs_3_ = bf16[1,128,1536]{2,1,0:T(8,128)(2,1)S(1)} collective-permute-done((bf16[1,128,1536]{2,1,0:T(8,128)(2,1)}, bf16[1,128,1536]{2,1,0:T(8,128)(2,1)S(1)}, u32[]{:S(2)}, u32[]{:S(2)}) %collective-permute-start.1) | collective-permute-done | bytes 393248 | tf_op jit(solution)/shard_map/ppermute | solution.py:259
  23.2 0.0 collective-permute-start.4
  23.2 4.1 %collective-permute-done.2.refs_4_ = bf16[1,128,1536]{2,1,0:T(8,128)(2,1)S(1)} collective-permute-done((bf16[1,128,1536]{2,1,0:T(8,128)(2,1)}, bf16[1,128,1536]{2,1,0:T(8,128)(2,1)S(1)}, u32[]{:S(2)}, u32[]{:S(2)}) %collective-permute-start.2) | collective-permute-done | bytes 393248 | tf_op jit(solution)/shard_map/ppermute | solution.py:260
  27.3 0.0 collective-permute-start.5
  28.0 0.0 copy-start
  28.0 0.7 %copy-done = f32[4,1536]{1,0:T(4,128)S(1)} copy-done((f32[4,1536]{1,0:T(4,128)S(1)}, f32[4,1536]{1,0:T(4,128)}, u32[]{:S(2)}) %copy-start) | copy-done | bytes 24600
  28.7 0.0 copy-start.1
  28.7 0.7 %copy-done.1 = s32[1,1,3]{2,1,0:T(1,128)S(1)} copy-done((s32[1,1,3]{2,1,0:T(1,128)S(1)}, s32[1,1,3]{2,1,0:T(1,128)}, u32[]{:S(2)}) %copy-start.1) | copy-done | bytes 36
  29.4 1.8 %stage.1 = (bf16[1,128,1536]{2,1,0:T(8,128)(2,1)S(1)}, bf16[1,128,1536]{2,1,0:T(8,128)(2,1)S(1)}, bf16[1,128,1536]{2,1,0:T(8,128)(2,1)S(1)}, f32[1,1536]{1,0:T(1,128)S(1)}, f32[8,128]{1,0:T(8,128)S(1)}) custom-call(s32[1]{0:T(128)S(6)} %copy.10.step, s32[1,1,3]{2,1,0:T(1,128)S(1)} %copy-done.1, f32[4,1536]{1,0:T(4,128)S(1)} %copy-done, ...), custom_call_target="tpu_custom_call" | custom-call | bytes 2359296 | tf_op jit(solution)/shard_map/stage/pallas_call | solution.py:165
  31.2 0.4 collective-permute-done.3.refs_5_
  31.5 0.0 collective-permute-done.6.q_one
  31.5 0.0 collective-permute-done.7.q_two
  31.5 0.0 collective-permute-done.4.refs_6_
  31.5 0.0 collective-permute-done.5.refs_7_
  31.6 0.0 slice-start
  31.6 2.9 %shard_map.94 = (bf16[128,1152]{1,0:T(8,128)(2,1)S(1)}, bf16[128,1152]{1,0:T(8,128)(2,1)S(1)}) custom-call(bf16[1,128,1536]{2,1,0:T(8,128)(2,1)S(1)} %collective-permute-done.6.q_one, bf16[1,128,1536]{2,1,0:T(8,128)(2,1)S(1)} %collective-permute-done.7.q_two, bf16[1,128,1536]{2,1,0:T(8,128)(2,1)S(1)} %get-tuple-element.20.refs_0_, ...), custom_call_target="tpu_custom_call" | custom-call | flops 536870912 | bytes 3145728 | tf_op jit(solution)/shard_map/pallas_call | solution.py:185
  34.5 5.5 %collective-permute-start.10 = (bf16[128,1152]{1,0:T(8,128)(2,1)S(1)}, bf16[128,1152]{1,0:T(8,128)(2,1)S(1)}, u32[]{:S(2)}, u32[]{:S(2)}) collective-permute-start(bf16[128,1152]{1,0:T(8,128)(2,1)S(1)} %get-tuple-element.29), channel_id=1, source_target_pairs={{0,1},{1,0},{2,3},{3,2},{4,5},{5,4},{6,7},{7,6},{8,9},{9,8},{10,11... | collective-permute-start | bytes 884744 | tf_op jit(solution)/shard_map/ppermute | solution.py:273
  40.0 0.0 slice-start.1
  40.0 0.0 collective-permute-start.11
  40.0 1.6 %shard_map.92 = (bf16[128,640]{1,0:T(8,128)(2,1)S(1)}, bf16[128,640]{1,0:T(8,128)(2,1)S(1)}) custom-call(bf16[1,128,1536]{2,1,0:T(8,128)(2,1)S(1)} %collective-permute-done.6.q_one, bf16[1,128,1536]{2,1,0:T(8,128)(2,1)S(1)} %collective-permute-done.7.q_two, bf16[1,128,1536]{2,1,0:T(8,128)(2,1)S(1)} %get-tuple-element.20.refs_0_, ...), custom_call_target="tpu_custom_call" | custom-call | flops 268435456 | bytes 1572864 | tf_op jit(solution)/shard_map/pallas_call | solution.py:185
  41.5 0.2 collective-permute-start.8
  41.8 2.2 %collective-permute-start.9 = (bf16[128,640]{1,0:T(8,128)(2,1)S(1)}, bf16[128,640]{1,0:T(8,128)(2,1)S(1)}, u32[]{:S(2)}, u32[]{:S(2)}) collective-permute-start(bf16[128,640]{1,0:T(8,128)(2,1)S(1)} %get-tuple-element.25), channel_id=1, source_target_pairs={{0,16},{1,2},{2,1},{3,4},{4,3},{5,6},{6,5},{7,8},{8,7},{9,10},{10,... | collective-permute-start | bytes 491528 | tf_op jit(solution)/shard_map/ppermute | solution.py:274
  43.9 1.3 %shard_map.91 = (f32[128,512]{1,0:T(8,128)S(1)}, f32[128,128]{1,0:T(8,128)S(1)}) custom-call(bf16[1,128,1536]{2,1,0:T(8,128)(2,1)S(1)} %get-tuple-element.19.q, bf16[1,128,1536]{2,1,0:T(8,128)(2,1)S(1)} %get-tuple-element.20.refs_0_, bf16[1,128,1536]{2,1,0:T(8,128)(2,1)S(1)} %get-tuple-element.21.refs_1_, ...), custom_call_target="tpu_custom_call" | custom-call | flops 134217728 | bytes 1441792 | tf_op jit(solution)/shard_map/pallas_call | solution.py:197
  45.3 2.5 %shard_map.93 = (f32[128,1024]{1,0:T(8,128)S(1)}, f32[128,128]{1,0:T(8,128)S(1)}) custom-call(bf16[1,128,1536]{2,1,0:T(8,128)(2,1)S(1)} %get-tuple-element.19.q, bf16[1,128,1536]{2,1,0:T(8,128)(2,1)S(1)} %get-tuple-element.20.refs_0_, bf16[1,128,1536]{2,1,0:T(8,128)(2,1)S(1)} %get-tuple-element.21.refs_1_, ...), custom_call_target="tpu_custom_call" | custom-call | flops 268435456 | bytes 2883584 | tf_op jit(solution)/shard_map/pallas_call | solution.py:197
  47.8 0.1 collective-permute-done.10.one
  47.8 2.0 %collective-permute-done.11.two = bf16[128,1152]{1,0:T(8,128)(2,1)S(1)} collective-permute-done((bf16[128,1152]{1,0:T(8,128)(2,1)S(1)}, bf16[128,1152]{1,0:T(8,128)(2,1)S(1)}, u32[]{:S(2)}, u32[]{:S(2)}) %collective-permute-start.11) | collective-permute-done | bytes 294944 | tf_op jit(solution)/shard_map/ppermute | solution.py:274
  49.9 0.0 slice-done
  49.9 0.0 slice-done.1
  49.9 1.2 %shard_map.95.rest_1_ = f32[128,1536]{1,0:T(8,128)S(1)} custom-call(f32[8,128]{1,0:T(8,128)S(1)} %get-tuple-element.18.bias, f32[128,1024]{1,0:T(8,128)S(1)} %get-tuple-element.27.own, f32[128,128]{1,0:T(8,128)S(1)} %get-tuple-element.28.own_lse, bf16[128,1152]{1,0:T(8,128)(2,1)S(1)} %collective-permute-done.10.one, ...), custom_call_target="tpu_custom_call" | custom-call | flops 402653184 | bytes 4718592 | tf_op jit(solution)/shard_map/pallas_call | solution.py:216
  51.1 0.0 collective-permute-done.8.one
  51.1 1.0 %collective-permute-done.9.two = bf16[128,640]{1,0:T(8,128)(2,1)S(1)} collective-permute-done((bf16[128,640]{1,0:T(8,128)(2,1)S(1)}, bf16[128,640]{1,0:T(8,128)(2,1)S(1)}, u32[]{:S(2)}, u32[]{:S(2)}) %collective-permute-start.9) | collective-permute-done | bytes 163872 | tf_op jit(solution)/shard_map/ppermute | solution.py:274
  52.1 1.6 %shard_map.96 = bf16[1,128,1536]{2,1,0:T(8,128)(2,1)} custom-call(f32[8,128]{1,0:T(8,128)S(1)} %get-tuple-element.18.bias, f32[128,512]{1,0:T(8,128)S(1)} %get-tuple-element.22.own, f32[128,128]{1,0:T(8,128)S(1)} %get-tuple-element.23.own_lse, bf16[128,640]{1,0:T(8,128)(2,1)S(1)} %collective-permute-done.8.one, ...), custom_call_target="tpu_custom_call" | custom-call | flops 201326592 | bytes 3145728 | tf_op jit(solution)/shard_map/pallas_call | solution.py:216
  (1 shorter events, 0.0 us)
Async XLA Ops:
  0.0 15.9 %collective-permute-start = (bf16[1,128,1536]{2,1,0:T(8,128)(2,1)}, bf16[1,128,1536]{2,1,0:T(8,128)(2,1)S(1)}, u32[]{:S(2)}, u32[]{:S(2)}) collective-permute-start(bf16[1,128,1536]{2,1,0:T(8,128)(2,1)} %param.12), channel_id=1, source_target_pairs={{0,32},{16,48},{32,64},{48,80},{64,96},{80,112},{96,128},{112,144}... | collective-permute-start | bytes 1179656 | tf_op jit(solution)/shard_map/ppermute | solution.py:258
  2.1 21.1 %collective-permute-start.1 = (bf16[1,128,1536]{2,1,0:T(8,128)(2,1)}, bf16[1,128,1536]{2,1,0:T(8,128)(2,1)S(1)}, u32[]{:S(2)}, u32[]{:S(2)}) collective-permute-start(bf16[1,128,1536]{2,1,0:T(8,128)(2,1)} %param.13), channel_id=1, source_target_pairs={{0,32},{16,48},{32,64},{48,80},{64,96},{80,112},{96,128},{112,144}... | collective-permute-start | bytes 1179656 | tf_op jit(solution)/shard_map/ppermute | solution.py:259
  4.5 22.8 %collective-permute-start.2 = (bf16[1,128,1536]{2,1,0:T(8,128)(2,1)}, bf16[1,128,1536]{2,1,0:T(8,128)(2,1)S(1)}, u32[]{:S(2)}, u32[]{:S(2)}) collective-permute-start(bf16[1,128,1536]{2,1,0:T(8,128)(2,1)} %param.12), channel_id=1, source_target_pairs={{0,16},{16,64},{32,48},{48,96},{64,80},{80,128},{96,112},{112,160}... | collective-permute-start | bytes 1179656 | tf_op jit(solution)/shard_map/ppermute | solution.py:260
  4.5 27.0 %collective-permute-start.3 = (bf16[1,128,1536]{2,1,0:T(8,128)(2,1)}, bf16[1,128,1536]{2,1,0:T(8,128)(2,1)S(1)}, u32[]{:S(2)}, u32[]{:S(2)}) collective-permute-start(bf16[1,128,1536]{2,1,0:T(8,128)(2,1)} %param.13), channel_id=1, source_target_pairs={{0,16},{16,64},{32,48},{48,96},{64,80},{80,128},{96,112},{112,160}... | collective-permute-start | bytes 1179656 | tf_op jit(solution)/shard_map/ppermute | solution.py:261
  6.2 25.3 %collective-permute-start.6 = (bf16[1,128,1536]{2,1,0:T(8,128)(2,1)}, bf16[1,128,1536]{2,1,0:T(8,128)(2,1)S(1)}, u32[]{:S(2)}, u32[]{:S(2)}) collective-permute-start(bf16[1,128,1536]{2,1,0:T(8,128)(2,1)} %q.1), channel_id=1, source_target_pairs={{0,1},{1,0},{2,3},{3,2},{4,5},{5,4},{6,7},{7,6},{8,9},{9,8},{10,11... | collective-permute-start | bytes 1179656 | tf_op jit(solution)/shard_map/ppermute | solution.py:262
  15.9 15.6 %collective-permute-start.7 = (bf16[1,128,1536]{2,1,0:T(8,128)(2,1)}, bf16[1,128,1536]{2,1,0:T(8,128)(2,1)S(1)}, u32[]{:S(2)}, u32[]{:S(2)}) collective-permute-start(bf16[1,128,1536]{2,1,0:T(8,128)(2,1)} %q.1), channel_id=1, source_target_pairs={{0,16},{1,2},{2,1},{3,4},{4,3},{5,6},{6,5},{7,8},{8,7},{9,10},{10,... | collective-permute-start | bytes 1179656 | tf_op jit(solution)/shard_map/ppermute | solution.py:263
  23.2 8.3 %collective-permute-start.4 = (bf16[1,128,1536]{2,1,0:T(8,128)(2,1)S(1)}, bf16[1,128,1536]{2,1,0:T(8,128)(2,1)S(1)}, u32[]{:S(2)}, u32[]{:S(2)}) collective-permute-start(bf16[1,128,1536]{2,1,0:T(8,128)(2,1)S(1)} %collective-permute-done.refs_2_), channel_id=1, source_target_pairs={{0,16},{16,0},{32,48},{48,32},{64,80},{80,64},{96,112},{112,96},{1... | collective-permute-start | bytes 1179656 | tf_op jit(solution)/shard_map/ppermute | solution.py:264
  27.3 4.2 %collective-permute-start.5 = (bf16[1,128,1536]{2,1,0:T(8,128)(2,1)S(1)}, bf16[1,128,1536]{2,1,0:T(8,128)(2,1)S(1)}, u32[]{:S(2)}, u32[]{:S(2)}) collective-permute-start(bf16[1,128,1536]{2,1,0:T(8,128)(2,1)S(1)} %collective-permute-done.1.refs_3_), channel_id=1, source_target_pairs={{0,16},{16,0},{32,48},{48,32},{64,80},{80,64},{96,112},{112,96},{1... | collective-permute-start | bytes 1179656 | tf_op jit(solution)/shard_map/ppermute | solution.py:265
  28.0 0.7 %copy-start = (f32[4,1536]{1,0:T(4,128)S(1)}, f32[4,1536]{1,0:T(4,128)}, u32[]{:S(2)}) copy-start(f32[4,1536]{1,0:T(4,128)} %gate.1) | copy-start | bytes 73732
  28.7 0.7 %copy-start.1 = (s32[1,1,3]{2,1,0:T(1,128)S(1)}, s32[1,1,3]{2,1,0:T(1,128)}, u32[]{:S(2)}) copy-start(s32[1,1,3]{2,1,0:T(1,128)} %mask.1) | copy-start | bytes 40
  31.6 18.3 %slice-start = ((s8[4718592]{0:T(1024)(128)(4,1)}), s8[4194304]{0:T(1024)(128)(4,1)S(1)}, s32[]{:S(2)}) async-start(s8[4718592]{0:T(1024)(128)(4,1)} %bitcast), calls=%async_computation | async-start | bytes 8388608
  34.5 13.3 %collective-permute-start.10 = (bf16[128,1152]{1,0:T(8,128)(2,1)S(1)}, bf16[128,1152]{1,0:T(8,128)(2,1)S(1)}, u32[]{:S(2)}, u32[]{:S(2)}) collective-permute-start(bf16[128,1152]{1,0:T(8,128)(2,1)S(1)} %get-tuple-element.29), channel_id=1, source_target_pairs={{0,1},{1,0},{2,3},{3,2},{4,5},{5,4},{6,7},{7,6},{8,9},{9,8},{10,11... | collective-permute-start | bytes 884744 | tf_op jit(solution)/shard_map/ppermute | solution.py:273
  40.0 9.9 %slice-start.1 = ((s8[4718592]{0:T(1024)(128)(4,1)}), s8[524288]{0:T(1024)(128)(4,1)S(1)}, s32[]{:S(2)}) async-start(s8[4718592]{0:T(1024)(128)(4,1)} %bitcast), calls=%async_computation.1 | async-start | bytes 1048576
  40.0 9.9 %collective-permute-start.11 = (bf16[128,1152]{1,0:T(8,128)(2,1)S(1)}, bf16[128,1152]{1,0:T(8,128)(2,1)S(1)}, u32[]{:S(2)}, u32[]{:S(2)}) collective-permute-start(bf16[128,1152]{1,0:T(8,128)(2,1)S(1)} %get-tuple-element.30), channel_id=1, source_target_pairs={{0,16},{1,2},{2,1},{3,4},{4,3},{5,6},{6,5},{7,8},{8,7},{9,10},{10,... | collective-permute-start | bytes 884744 | tf_op jit(solution)/shard_map/ppermute | solution.py:274
  41.5 9.6 %collective-permute-start.8 = (bf16[128,640]{1,0:T(8,128)(2,1)S(1)}, bf16[128,640]{1,0:T(8,128)(2,1)S(1)}, u32[]{:S(2)}, u32[]{:S(2)}) collective-permute-start(bf16[128,640]{1,0:T(8,128)(2,1)S(1)} %get-tuple-element.24), channel_id=1, source_target_pairs={{0,1},{1,0},{2,3},{3,2},{4,5},{5,4},{6,7},{7,6},{8,9},{9,8},{10,11... | collective-permute-start | bytes 491528 | tf_op jit(solution)/shard_map/ppermute | solution.py:273
  41.8 10.4 %collective-permute-start.9 = (bf16[128,640]{1,0:T(8,128)(2,1)S(1)}, bf16[128,640]{1,0:T(8,128)(2,1)S(1)}, u32[]{:S(2)}, u32[]{:S(2)}) collective-permute-start(bf16[128,640]{1,0:T(8,128)(2,1)S(1)} %get-tuple-element.25), channel_id=1, source_target_pairs={{0,16},{1,2},{2,1},{3,4},{4,3},{5,6},{6,5},{7,8},{8,7},{9,10},{10,... | collective-permute-start | bytes 491528 | tf_op jit(solution)/shard_map/ppermute | solution.py:274
where the time goes:
time: 53.9 us; the launch traced here: 53.7 us
  waiting for transfers between devices  22.5 us (42%)
  starting transfers between devices  16.1 us (30%)
  Pallas kernels  12.9 us (24%)
  local copies, waits for them, and re-layouts  1.4 us (3%)
  between operations  0.75 us (1%)
    ppermute x1, waiting for transfers between devices, on_device(): k2 = lax.ppermute(key_clean, 'tm', two_back)  8.65 us
    ppermute x1, waiting for transfers between devices, on_device(): v2 = lax.ppermute(value_clean, 'tm', two_back)  6.29 us
    ppermute x2, starting transfers between devices, on_device(): from_one = lax.ppermute(to_one, 'space', one)  5.7 us
    pallas_call x2, Pallas kernels, neighbour(): pl.pallas_call(functools.partial(neighbour_kernel, first, heads), out_sha...  4.47 us
    ppermute x1, waiting for transfers between devices, on_device(): ks = lax.ppermute(key_clean, 'tm', side)  4.11 us
    pallas_call x2, Pallas kernels, own(): pl.pallas_call(functools.partial(own_kernel, first, heads), out_shape=(ja...  3.83 us
    ppermute x2, waiting for transfers between devices, on_device(): from_two = lax.ppermute(to_two, both, two)  3.03 us
    pallas_call x2, Pallas kernels, merge(): pl.pallas_call(functools.partial(merge_kernel, first, heads, has_sum, las...  2.81 us
  transfers between devices with their start and end apart: 12, of which 7 were waited for; matrix products, arithmetic and copies ran while one was open for 0% of the time, Pallas kernels for 16%

commit v1 on v0

--- a/solution.py
+++ b/solution.py
@@ -44,9 +44,32 @@
     return accum * (1.0 / total), peak + jnp.log2(total)
 
 
-def chunk_blocks(h, blocks):
-    cols = slice(h * HEAD, (h + 1) * HEAD)
-    return cols, [r[0, :, cols] for r in blocks[0::2]], [r[0, :, cols] for r in blocks[1::2]]
+def chunk_blocks(first, heads, h, kn, vn, packs):
+    cols = slice((first + h) * HEAD, (first + h + 1) * HEAD)
+    key_cols = slice(h * HEAD, (h + 1) * HEAD)
+    value_cols = slice((heads + h) * HEAD, (heads + h + 1) * HEAD)
+    keys = [kn[0, :, cols]] + [p[:, key_cols] for p in packs]
+    values = [vn[0, :, cols]] + [p[:, value_cols] for p in packs]
+    return cols, keys, values
+
+
+def pack_kernel(first, heads, key, value, out, sems):
+    width = heads * HEAD
+    rows = TILE // PACK_PARTS
+    copies = []
+    for part in range(PACK_PARTS):
+        for i, source in enumerate((key, value)):
+            copies.append(
+                pltpu.make_async_copy(
+                    source.at[0, pl.ds(part * rows, rows), pl.ds(first * HEAD, width)],
+                    out.at[pl.ds(part * rows, rows), pl.ds(i * width, width)],
+                    sems.at[part, i],
+                )
+            )
+    for copy in copies:
+        copy.start()
+    for copy in copies:
+        copy.wait()
 
 
 def stage_kernel(tiles_all, step, mask, gate, q, kn, vn, q_out, kn_out, vn_out, gate_out, bias_out, sems):
@@ -70,71 +93,85 @@
         copy.wait()
 
 
-def neighbour_kernel(first, heads, q_one, q_two, *refs):
-    blocks, (to_one, to_two) = refs[:8], refs[8:]
+def at_meeting(half):
+    tile = lax.axis_index("space")
+    odd = lax.rem(lax.axis_index("tm"), 2) == 1
+    return odd & ((tile == half - 1) | (tile == half))
+
+
+def neighbour_kernel(half, first, heads, q_one, q_two, q_meet, kn, vn, *refs):
+    packs, (to_one, to_two) = refs[:3], refs[3:]
     biases = [None] + past_bias(lax.axis_index("tm"))
     lane = lax.broadcasted_iota(jnp.int32, (2 * TILE, HEAD), 1)
     stats = jnp.zeros((2 * TILE, HEAD), jnp.float32)
-    width = heads * HEAD
+    meeting = at_meeting(half)
     for h in range(heads):
-        cols, keys, values = chunk_blocks(first + h, blocks)
-        q = jnp.concatenate([q_one[0, :, cols], q_two[0, :, cols]], axis=0)
+        cols, keys, values = chunk_blocks(first, heads, h, kn, vn, packs)
+        second = jnp.where(meeting, q_meet[0, :, cols], q_two[0, :, cols])
+        q = jnp.concatenate([q_one[0, :, cols], second], axis=0)
         part, lse = head_partial(q, keys, values, biases)
         part = part.astype(jnp.bfloat16)
         here = slice(h * HEAD, (h + 1) * HEAD)
-        to_one[:, here] = part[:TILE]
-        to_two[:, here] = part[TILE:]
+        to_one[:TILE, here] = part[:TILE]
+        to_two[:TILE, here] = part[TILE:]
         stats = jnp.where(lane == h, lse, stats)
     first_part = stats.astype(jnp.bfloat16).astype(jnp.float32)
     rest = stats - first_part
     second_part = rest.astype(jnp.bfloat16).astype(jnp.float32)
     third_part = rest - second_part
-    packed = first_part + pltpu.roll(second_part, 16, 1) + pltpu.roll(third_part, 32, 1)
-    packed = packed.astype(jnp.bfloat16)
-    to_one[:, width:] = packed[:TILE]
-    to_two[:, width:] = packed[TILE:]
-
-
-def own_kernel(first, heads, q, *refs):
-    blocks, (out, out_lse) = refs[:8], refs[8:]
+    packed = first_part + pltpu.roll(second_part, 8, 1) + pltpu.roll(third_part, 16, 1)
+    for target, block in ((to_one, packed[:TILE]), (to_two, packed[TILE:])):
+        turned = block.T.astype(jnp.bfloat16)
+        for part in range(3):
+            target[TILE:, part * HEAD : (part + 1) * HEAD] = turned[part * 8 : (part + 1) * 8]
+        for part in range(3, heads):
+            target[TILE:, part * HEAD : (part + 1) * HEAD] = jnp.zeros((8, HEAD), jnp.bfloat16)
+
+
+def own_kernel(first, heads, start, count, q, kn, vn, *refs):
+    packs, (out, out_lse) = refs[:3], refs[3:]
     biases = [None] + past_bias(lax.axis_index("tm"))
     lane = lax.broadcasted_iota(jnp.int32, (TILE, HEAD), 1)
     stats = jnp.zeros((TILE, HEAD), jnp.float32)
-    for h in range(heads):
-        cols, keys, values = chunk_blocks(first + h, blocks)
+    for h in range(start, start + count):
+        cols, keys, values = chunk_blocks(first, heads, h, kn, vn, packs)
         part, lse = head_partial(q[0, :, cols], keys, values, biases)
-        out[:, h * HEAD : (h + 1) * HEAD] = part
+        out[:, (h - start) * HEAD : (h - start + 1) * HEAD] = part
         stats = jnp.where(lane == h, lse, stats)
     out_lse[...] = stats
 
 
-def unpacked(block):
-    packed = block.astype(jnp.float32)
-    return packed + pltpu.roll(packed, HEAD - 16, 1) + pltpu.roll(packed, HEAD - 32, 1)
-
-
-def merge_kernel(first, heads, has_sum, last, bias, own, own_lse, one, two, weight, *rest):
+def unpacked(rows):
+    parts = rows.astype(jnp.float32)
+    lse = parts[:, :HEAD] + parts[:, HEAD : 2 * HEAD] + parts[:, 2 * HEAD : 3 * HEAD]
+    return jnp.concatenate([lse, jnp.zeros((HEAD - 8, HEAD), jnp.float32)], axis=0).T
+
+
+def merge_kernel(first, heads, parts, has_sum, last, bias, one, two, weight, *rest):
     rest = list(rest)
+    own = [rest.pop(0) for _ in range(parts)]
+    own_lse = [rest.pop(0) for _ in range(parts)]
     gate = rest.pop(0) if last else None
     before = rest.pop(0) if has_sum else None
     out, attended = rest
     width = heads * HEAD
-    lse_own = own_lse[...]
-    lse_one = unpacked(one[:, width:]) + bias[0:1, :]
-    lse_two = unpacked(two[:, width:]) + bias[1:2, :]
+    lse_own = functools.reduce(jnp.add, [r[...] for r in own_lse])
+    lse_one = unpacked(one[TILE:, : 3 * HEAD]) + bias[0:1, :]
+    lse_two = unpacked(two[TILE:, : 3 * HEAD]) + bias[1:2, :]
     peak = jnp.maximum(jnp.maximum(lse_own, lse_one), lse_two)
     w_own = jnp.exp2(lse_own - peak)
     w_one = jnp.exp2(lse_one - peak)
     w_two = jnp.exp2(lse_two - peak)
     inv = 1.0 / (w_own + w_one + w_two)
     w_own, w_one, w_two = w_own * inv, w_one * inv, w_two * inv
+    count = heads // parts
     for h in range(heads):
         cols = slice(h * HEAD, (h + 1) * HEAD)
         lane = slice(h, h + 1)
         mixed = (
-            w_own[:, lane] * own[:, cols]
-            + w_one[:, lane] * one[:, cols].astype(jnp.float32)
-            + w_two[:, lane] * two[:, cols].astype(jnp.float32)
+            w_own[:, lane] * own[h // count][:, (h % count) * HEAD : (h % count + 1) * HEAD]
+            + w_one[:, lane] * one[:TILE, cols].astype(jnp.float32)
+            + w_two[:, lane] * two[:TILE, cols].astype(jnp.float32)
         )
         attended[:, cols] = mixed.astype(jnp.bfloat16)
     att = attended[...]
@@ -154,10 +191,24 @@
 SMEM = pl.BlockSpec(memory_space=pltpu.SMEM)
 HBM = pl.BlockSpec(memory_space=pltpu.HBM)
 CHUNKS = ((0, 8), (8, 4))
+OWN_PARTS = (2, 1)
+PACK_PARTS = 1
 
 
 def cost(flops, moved, exps=0):
     return pl.CostEstimate(flops=flops, bytes_accessed=moved, transcendentals=exps)
+
+
+def pack(first, heads, key, value):
+    return pl.pallas_call(
+        functools.partial(pack_kernel, first, heads),
+        out_shape=jax.ShapeDtypeStruct((TILE, 2 * heads * HEAD), jnp.bfloat16),
+        in_specs=[HBM, HBM],
+        out_specs=VMEM,
+        scratch_shapes=[pltpu.SemaphoreType.DMA((PACK_PARTS, 2))],
+        cost_estimate=cost(0, 8 * TILE * heads * HEAD),
+        compiler_params=PARAMS,
+    )(*in_hbm(key, value))
 
 
 def stage(space_size, noise_step, tile_mask, step_gate, query, key_new, value_new):
@@ -180,41 +231,41 @@
     )(noise_step, tile_mask, step_gate, *in_hbm(query, key_new, value_new))
 
 
-def neighbour(first, heads, *args):
+def neighbour(half, first, heads, *args):
     width = heads * HEAD
     return pl.pallas_call(
-        functools.partial(neighbour_kernel, first, heads),
-        out_shape=(jax.ShapeDtypeStruct((TILE, width + HEAD), jnp.bfloat16),) * 2,
-        in_specs=[VMEM] * 10,
+        functools.partial(neighbour_kernel, half, first, heads),
+        out_shape=(jax.ShapeDtypeStruct((TILE + 8, width), jnp.bfloat16),) * 2,
+        in_specs=[VMEM] * 8,
         out_specs=(VMEM, VMEM),
         cost_estimate=cost(4 * 256 * 512 * width, 24 * TILE * width, heads * 256 * 512),
         compiler_params=PARAMS,
     )(*args)
 
 
-def own(first, heads, *args):
-    width = heads * HEAD
-    return pl.pallas_call(
-        functools.partial(own_kernel, first, heads),
+def own(first, heads, start, count, *args):
+    width = count * HEAD
+    return pl.pallas_call(
+        functools.partial(own_kernel, first, heads, start, count),
         out_shape=(
             jax.ShapeDtypeStruct((TILE, width), jnp.float32),
             jax.ShapeDtypeStruct((TILE, HEAD), jnp.float32),
         ),
-        in_specs=[VMEM] * 9,
+        in_specs=[VMEM] * 6,
         out_specs=(VMEM, VMEM),
-        cost_estimate=cost(4 * 128 * 512 * width, 22 * TILE * width, heads * 128 * 512),
+        cost_estimate=cost(4 * 128 * 512 * width, 22 * TILE * width, count * 128 * 512),
         compiler_params=PARAMS,
     )(*args)
 
 
-def merge(first, heads, has_sum, last, *args):
+def merge(first, heads, parts, has_sum, last, *args):
     width = heads * HEAD
     if last:
         result = jax.ShapeDtypeStruct((1, TILE, D), jnp.bfloat16)
     else:
         result = jax.ShapeDtypeStruct((TILE, D), jnp.float32)
     return pl.pallas_call(
-        functools.partial(merge_kernel, first, heads, has_sum, last),
+        functools.partial(merge_kernel, first, heads, parts, has_sum, last),
         out_shape=result,
         in_specs=[VMEM] * len(args),
         out_specs=VMEM,
@@ -254,30 +305,53 @@
             target = (t, to) if inside else (swap[t][1], s)
             two.append((t * space_size + s, target[0] * space_size + target[1]))
     both = ("tm", "space")
-
-    k2 = lax.ppermute(key_clean, "tm", two_back)
-    v2 = lax.ppermute(value_clean, "tm", two_back)
-    ks = lax.ppermute(key_clean, "tm", side)
-    vs = lax.ppermute(value_clean, "tm", side)
+    half = space_size // 2
+    low, high, end = half - 1, half, space_size - 1
+    hop = {divmod(a, space_size): divmod(b, space_size) for a, b in two}
+    across = {}
+    for t in range(tm_size):
+        for s in range(space_size):
+            across[t, s] = (swap[t][1], s)
+    for t in range(0, tm_size, 2):
+        hop[t, 0], hop[t, end] = (t + 1, low), (t + 1, high)
+        hop[t + 1, 0], hop[t + 1, end] = (t, 0), (t, end)
+        hop[t + 1, low], hop[t + 1, high] = (t + 1, 0), (t + 1, end)
+        across[t + 1, 0], across[t + 1, end] = (t + 1, high), (t + 1, low)
+        across[t, low], across[t, high] = (t, 0), (t, end)
+    hop = [(a[0] * space_size + a[1], b[0] * space_size + b[1]) for a, b in hop.items()]
+    across = [(a[0] * space_size + a[1], b[0] * space_size + b[1]) for a, b in across.items()]
+
+    crossing = []
+    for first, heads in CHUNKS:
+        packed = pack(first, heads, key_clean, value_clean)
+        pair = lax.ppermute(packed, "tm", two_back), lax.ppermute(packed, "tm", side)
+        crossing.append(pair)
     q_one = lax.ppermute(query, "space", one)
-    q_two = lax.ppermute(query, both, two)
-    kx = lax.ppermute(k2, "tm", swap)
-    vx = lax.ppermute(v2, "tm", swap)
+    q_two = lax.ppermute(query, both, hop)
+    q_meet = lax.ppermute(q_two, both, across)
     q, kn, vn, gate_row, bias = stage(
         space_size, noise_step, tile_mask, step_gate, query, key_new, value_new
     )
-    blocks = (kn, vn, k2, v2, ks, vs, kx, vx)
     total = None
     for i, (first, heads) in enumerate(CHUNKS):
-        to_one, to_two = neighbour(first, heads, q_one, q_two, *blocks)
+        two_ago, aside = crossing[i]
+        swapped = lax.ppermute(two_ago, "tm", swap)
+        blocks = (kn, vn, two_ago, aside, swapped)
+        to_one, to_two = neighbour(half, first, heads, q_one, q_two, q_meet, *blocks)
         from_one = lax.ppermute(to_one, "space", one)
+        last = i == len(CHUNKS) - 1
         from_two = lax.ppermute(to_two, both, two)
-        mine, mine_lse = own(first, heads, q, *blocks)
+        parts = OWN_PARTS[i]
+        mine = []
+        for j in range(parts):
+            count = heads // parts
+            mine.append(own(first, heads, j * count, count, q, *blocks))
         last = i == len(CHUNKS) - 1
-        args = [bias, mine, mine_lse, from_one, from_two, out_weight]
+        args = [bias, from_one, from_two, out_weight]
+        args += [m[0] for m in mine] + [m[1] for m in mine]
         args += [gate_row] if last else []
         args += [total] if i > 0 else []
-        total = merge(first, heads, i > 0, last, *args)
+        total = merge(first, heads, parts, i > 0, last, *args)
     return total
 
 

time: 53.9 us -> 62.9 us (1.17)
  the two profiles are of different devices: /device:TPU:194 before, /device:TPU:2 now
where the time goes in v1:
time: 62.9 us; the launch traced here: 62.7 us
  starting transfers between devices  23.7 us (38%)
  waiting for transfers between devices  21.2 us (34%)
  Pallas kernels  15.6 us (25%)
  local copies, waits for them, and re-layouts  1.4 us (2%)
  between operations  0.78 us (1%)
    ppermute x2, waiting for transfers between devices, on_device(): lax.ppermute(packed, 'tm', two_back)  18.5 us
    ppermute x1, starting transfers between devices, on_device(): q_meet = lax.ppermute(q_two, both, across)  8.14 us
    ppermute x1, starting transfers between devices, on_device(): q_two = lax.ppermute(query, both, hop)  6.73 us
    pallas_call x2, Pallas kernels, neighbour(): pl.pallas_call(functools.partial(neighbour_kernel, half, first, heads), o...  4.64 us
    pallas_call x3, Pallas kernels, own(): pl.pallas_call(functools.partial(own_kernel, first, heads, start, count),...  3.99 us
    pallas_call x2, Pallas kernels, merge(): pl.pallas_call(functools.partial(merge_kernel, first, heads, parts, has_s...  2.91 us
    ppermute x2, starting transfers between devices, on_device(): from_two = lax.ppermute(to_two, both, two)  2.73 us
    ppermute x2, waiting for transfers between devices, on_device(): from_two = lax.ppermute(to_two, both, two)  2.7 us
  transfers between devices with their start and end apart: 13, of which 4 were waited for; matrix products, arithmetic and copies ran while one was open for 0% of the time, Pallas kernels for 21%

profile of v1, /device:TPU:2, one launch (start us, length us, event | category | flops | bytes accessed | tf_op | source)
XLA Modules:
  0.0 62.7 jit_solution(17013451759106220471)
XLA Ops:
  0.0 1.0 %shard_map.94 = bf16[128,2048]{1,0:T(8,128)(2,1)S(1)} custom-call(bf16[1,128,1536]{2,1,0:T(8,128)(2,1)} %key.3, bf16[1,128,1536]{2,1,0:T(8,128)(2,1)} %value.3), custom_call_target="tpu_custom_call" | custom-call | bytes 1048576 | tf_op jit(solution)/shard_map/pallas_call | solution.py:203
  1.1 2.2 %collective-permute-start.8 = (bf16[128,2048]{1,0:T(8,128)(2,1)S(1)}, bf16[128,2048]{1,0:T(8,128)(2,1)S(1)}, u32[]{:S(2)}, u32[]{:S(2)}) collective-permute-start(bf16[128,2048]{1,0:T(8,128)(2,1)S(1)} %shard_map.94), channel_id=1, source_target_pairs={{0,32},{16,48},{32,64},{48,80},{64,96},{80,112},{96,128},{112,144}... | collective-permute-start | bytes 1572872 | tf_op jit(solution)/shard_map/ppermute | solution.py:327
  3.3 6.7 %collective-permute-start.1 = (bf16[1,128,1536]{2,1,0:T(8,128)(2,1)}, bf16[1,128,1536]{2,1,0:T(8,128)(2,1)S(1)}, u32[]{:S(2)}, u32[]{:S(2)}) collective-permute-start(bf16[1,128,1536]{2,1,0:T(8,128)(2,1)} %q.1), channel_id=1, source_target_pairs={{0,23},{1,2},{2,1},{3,4},{4,3},{5,6},{6,5},{7,8},{8,7},{9,10},{10,... | collective-permute-start | bytes 1179656 | tf_op jit(solution)/shard_map/ppermute | solution.py:330
  10.0 0.0 collective-permute-start.9
  10.0 8.5 %collective-permute-done.8.refs_0_ = bf16[128,2048]{1,0:T(8,128)(2,1)S(1)} collective-permute-done((bf16[128,2048]{1,0:T(8,128)(2,1)S(1)}, bf16[128,2048]{1,0:T(8,128)(2,1)S(1)}, u32[]{:S(2)}, u32[]{:S(2)}) %collective-permute-start.8) | collective-permute-done | bytes 524320 | tf_op jit(solution)/shard_map/ppermute | solution.py:327
  18.5 0.0 collective-permute-start.10
  18.5 1.9 %collective-permute-start = (bf16[1,128,1536]{2,1,0:T(8,128)(2,1)}, bf16[1,128,1536]{2,1,0:T(8,128)(2,1)S(1)}, u32[]{:S(2)}, u32[]{:S(2)}) collective-permute-start(bf16[1,128,1536]{2,1,0:T(8,128)(2,1)} %q.1), channel_id=1, source_target_pairs={{0,1},{1,0},{2,3},{3,2},{4,5},{5,4},{6,7},{7,6},{8,9},{9,8},{10,11... | collective-permute-start | bytes 1179656 | tf_op jit(solution)/shard_map/ppermute | solution.py:329
  20.4 0.0 collective-permute-done.1.q_two
  20.4 8.1 %collective-permute-start.2 = (bf16[1,128,1536]{2,1,0:T(8,128)(2,1)S(1)}, bf16[1,128,1536]{2,1,0:T(8,128)(2,1)S(1)}, u32[]{:S(2)}, u32[]{:S(2)}) collective-permute-start(bf16[1,128,1536]{2,1,0:T(8,128)(2,1)S(1)} %collective-permute-done.1.q_two), channel_id=1, source_target_pairs={{0,16},{1,17},{2,18},{3,19},{4,20},{5,21},{6,22},{7,0},{8,15},{9,2... | collective-permute-start | bytes 1179656 | tf_op jit(solution)/shard_map/ppermute | solution.py:331
  28.6 1.0 %shard_map.91 = bf16[128,1024]{1,0:T(8,128)(2,1)S(1)} custom-call(bf16[1,128,1536]{2,1,0:T(8,128)(2,1)} %key.3, bf16[1,128,1536]{2,1,0:T(8,128)(2,1)} %value.3), custom_call_target="tpu_custom_call" | custom-call | bytes 524288 | tf_op jit(solution)/shard_map/pallas_call | solution.py:203
  29.6 0.1 collective-permute-start.3
  29.7 10.0 %collective-permute-done.3.refs_0_ = bf16[128,1024]{1,0:T(8,128)(2,1)S(1)} collective-permute-done((bf16[128,1024]{1,0:T(8,128)(2,1)S(1)}, bf16[128,1024]{1,0:T(8,128)(2,1)S(1)}, u32[]{:S(2)}, u32[]{:S(2)}) %collective-permute-start.3) | collective-permute-done | bytes 262176 | tf_op jit(solution)/shard_map/ppermute | solution.py:327
  39.6 0.0 collective-permute-start.4
  39.6 0.0 collective-permute-done.q_one
  39.6 0.0 collective-permute-start.5
  40.3 0.0 copy-start
  40.3 0.7 %copy-done = f32[4,1536]{1,0:T(4,128)S(1)} copy-done((f32[4,1536]{1,0:T(4,128)S(1)}, f32[4,1536]{1,0:T(4,128)}, u32[]{:S(2)}) %copy-start) | copy-done | bytes 24600
  41.0 0.0 copy-start.1
  41.0 0.7 %copy-done.1 = s32[1,1,3]{2,1,0:T(1,128)S(1)} copy-done((s32[1,1,3]{2,1,0:T(1,128)S(1)}, s32[1,1,3]{2,1,0:T(1,128)}, u32[]{:S(2)}) %copy-start.1) | copy-done | bytes 36
  41.7 0.0 slice-start
  41.7 2.1 %stage.1 = (bf16[1,128,1536]{2,1,0:T(8,128)(2,1)S(1)}, bf16[1,128,1536]{2,1,0:T(8,128)(2,1)S(1)}, bf16[1,128,1536]{2,1,0:T(8,128)(2,1)S(1)}, f32[1,1536]{1,0:T(1,128)S(1)}, f32[8,128]{1,0:T(8,128)S(1)}) custom-call(s32[1]{0:T(128)S(6)} %copy.10.step, s32[1,1,3]{2,1,0:T(1,128)S(1)} %copy-done.1, f32[4,1536]{1,0:T(4,128)S(1)} %copy-done, ...), custom_call_target="tpu_custom_call" | custom-call | bytes 2359296 | tf_op jit(solution)/shard_map/stage/pallas_call | solution.py:216
  43.8 0.0 collective-permute-done.9.refs_1_
  43.8 0.0 collective-permute-done.2.q_meet
  43.8 0.0 collective-permute-done.10.refs_2_
  43.8 3.0 %shard_map.95 = (bf16[136,1024]{1,0:T(8,128)(2,1)S(1)}, bf16[136,1024]{1,0:T(8,128)(2,1)S(1)}) custom-call(bf16[1,128,1536]{2,1,0:T(8,128)(2,1)S(1)} %collective-permute-done.q_one, bf16[1,128,1536]{2,1,0:T(8,128)(2,1)S(1)} %collective-permute-done.1.q_two, bf16[1,128,1536]{2,1,0:T(8,128)(2,1)S(1)} %collective-permute-done.2.q_meet, ...), custom_call_target="tpu_custom_call" | custom-call | flops 536870912 | bytes 3145728 | tf_op jit(solution)/shard_map/pallas_call | solution.py:236
  46.8 0.1 collective-permute-start.11
  46.9 0.0 slice-start.1
  46.9 0.2 collective-permute-start.12
  47.1 0.0 collective-permute-done.4.refs_1_
  47.1 0.0 collective-permute-done.5.refs_2_
  47.1 1.6 %shard_map.92 = (bf16[136,512]{1,0:T(8,128)(2,1)S(1)}, bf16[136,512]{1,0:T(8,128)(2,1)S(1)}) custom-call(bf16[1,128,1536]{2,1,0:T(8,128)(2,1)S(1)} %collective-permute-done.q_one, bf16[1,128,1536]{2,1,0:T(8,128)(2,1)S(1)} %collective-permute-done.1.q_two, bf16[1,128,1536]{2,1,0:T(8,128)(2,1)S(1)} %collective-permute-done.2.q_meet, ...), custom_call_target="tpu_custom_call" | custom-call | flops 268435456 | bytes 1572864 | tf_op jit(solution)/shard_map/pallas_call | solution.py:236
  48.8 1.8 %collective-permute-start.6 = (bf16[136,512]{1,0:T(8,128)(2,1)S(1)}, bf16[136,512]{1,0:T(8,128)(2,1)S(1)}, u32[]{:S(2)}, u32[]{:S(2)}) collective-permute-start(bf16[136,512]{1,0:T(8,128)(2,1)S(1)} %get-tuple-element.23), channel_id=1, source_target_pairs={{0,1},{1,0},{2,3},{3,2},{4,5},{5,4},{6,7},{7,6},{8,9},{9,8},{10,11... | collective-permute-start | bytes 417800 | tf_op jit(solution)/shard_map/ppermute | solution.py:341
  50.6 2.5 %collective-permute-start.7 = (bf16[136,512]{1,0:T(8,128)(2,1)S(1)}, bf16[136,512]{1,0:T(8,128)(2,1)S(1)}, u32[]{:S(2)}, u32[]{:S(2)}) collective-permute-start(bf16[136,512]{1,0:T(8,128)(2,1)S(1)} %get-tuple-element.24), channel_id=1, source_target_pairs={{0,16},{1,2},{2,1},{3,4},{4,3},{5,6},{6,5},{7,8},{8,7},{9,10},{10,... | collective-permute-start | bytes 417800 | tf_op jit(solution)/shard_map/ppermute | solution.py:343
  53.1 1.3 %shard_map.93 = (f32[128,512]{1,0:T(8,128)S(1)}, f32[128,128]{1,0:T(8,128)S(1)}) custom-call(bf16[1,128,1536]{2,1,0:T(8,128)(2,1)S(1)} %get-tuple-element.25.q, bf16[1,128,1536]{2,1,0:T(8,128)(2,1)S(1)} %get-tuple-element.21.kn, bf16[1,128,1536]{2,1,0:T(8,128)(2,1)S(1)} %get-tuple-element.22.vn, bf16[128,1024]{1,0:T(8,128)(2,1)S(1)} %collective-permute-done.3.refs_0_, ...), custom_call_target="tpu_custom_call" | custom-call | flops 134217728 | bytes 1441792 | tf_op jit(solution)/shard_map/pallas_call | solution.py:248
  54.4 1.3 %shard_map.96 = (f32[128,512]{1,0:T(8,128)S(1)}, f32[128,128]{1,0:T(8,128)S(1)}) custom-call(bf16[1,128,1536]{2,1,0:T(8,128)(2,1)S(1)} %get-tuple-element.25.q, bf16[1,128,1536]{2,1,0:T(8,128)(2,1)S(1)} %get-tuple-element.21.kn, bf16[1,128,1536]{2,1,0:T(8,128)(2,1)S(1)} %get-tuple-element.22.vn, bf16[128,2048]{1,0:T(8,128)(2,1)S(1)} %collective-permute-done.8.refs_0_, ...), custom_call_target="tpu_custom_call" | custom-call | flops 134217728 | bytes 1441792 | tf_op jit(solution)/shard_map/pallas_call | solution.py:248
  55.8 1.3 %shard_map.97 = (f32[128,512]{1,0:T(8,128)S(1)}, f32[128,128]{1,0:T(8,128)S(1)}) custom-call(bf16[1,128,1536]{2,1,0:T(8,128)(2,1)S(1)} %get-tuple-element.25.q, bf16[1,128,1536]{2,1,0:T(8,128)(2,1)S(1)} %get-tuple-element.21.kn, bf16[1,128,1536]{2,1,0:T(8,128)(2,1)S(1)} %get-tuple-element.22.vn, bf16[128,2048]{1,0:T(8,128)(2,1)S(1)} %collective-permute-done.8.refs_0_, ...), custom_call_target="tpu_custom_call" | custom-call | flops 134217728 | bytes 1441792 | tf_op jit(solution)/shard_map/pallas_call | solution.py:248
  57.1 0.0 collective-permute-done.11.one
  57.1 1.5 %collective-permute-done.12.two = bf16[136,1024]{1,0:T(8,128)(2,1)S(1)} collective-permute-done((bf16[136,1024]{1,0:T(8,128)(2,1)S(1)}, bf16[136,1024]{1,0:T(8,128)(2,1)S(1)}, u32[]{:S(2)}, u32[]{:S(2)}) %collective-permute-start.12) | collective-permute-done | bytes 278560 | tf_op jit(solution)/shard_map/ppermute | solution.py:343
  58.6 0.0 slice-done
  58.6 0.0 slice-done.1
  58.6 1.3 %shard_map.98.rest_3_ = f32[128,1536]{1,0:T(8,128)S(1)} custom-call(f32[8,128]{1,0:T(8,128)S(1)} %get-tuple-element.20.bias, bf16[136,1024]{1,0:T(8,128)(2,1)S(1)} %collective-permute-done.11.one, bf16[136,1024]{1,0:T(8,128)(2,1)S(1)} %collective-permute-done.12.two, bf16[1536,1536]{1,0:T(8,128)(2,1)S(1)} %bitcast.1, ...), custom_call_target="tpu_custom_call" | custom-call | flops 402653184 | bytes 4718592 | tf_op jit(solution)/shard_map/pallas_call | solution.py:267
  59.9 0.0 collective-permute-done.6.one
  60.0 1.2 %collective-permute-done.7.two = bf16[136,512]{1,0:T(8,128)(2,1)S(1)} collective-permute-done((bf16[136,512]{1,0:T(8,128)(2,1)S(1)}, bf16[136,512]{1,0:T(8,128)(2,1)S(1)}, u32[]{:S(2)}, u32[]{:S(2)}) %collective-permute-start.7) | collective-permute-done | bytes 139296 | tf_op jit(solution)/shard_map/ppermute | solution.py:343
  61.1 1.6 %shard_map.99 = bf16[1,128,1536]{2,1,0:T(8,128)(2,1)} custom-call(f32[8,128]{1,0:T(8,128)S(1)} %get-tuple-element.20.bias, bf16[136,512]{1,0:T(8,128)(2,1)S(1)} %collective-permute-done.6.one, bf16[136,512]{1,0:T(8,128)(2,1)S(1)} %collective-permute-done.7.two, bf16[1536,1536]{1,0:T(8,128)(2,1)S(1)} %bitcast.1, f32[128,512]{1,0:T(8,128)S(1)} %get-tuple-element.26.rest_0_, ...), custom_call_target="tpu_custom_call" | custom-call | flops 201326592 | bytes 3145728 | tf_op jit(solution)/shard_map/pallas_call | solution.py:267
  (1 shorter events, 0.0 us)
Async XLA Ops:
  1.1 17.5 %collective-permute-start.8 = (bf16[128,2048]{1,0:T(8,128)(2,1)S(1)}, bf16[128,2048]{1,0:T(8,128)(2,1)S(1)}, u32[]{:S(2)}, u32[]{:S(2)}) collective-permute-start(bf16[128,2048]{1,0:T(8,128)(2,1)S(1)} %shard_map.94), channel_id=1, source_target_pairs={{0,32},{16,48},{32,64},{48,80},{64,96},{80,112},{96,128},{112,144}... | collective-permute-start | bytes 1572872 | tf_op jit(solution)/shard_map/ppermute | solution.py:327
  3.3 17.2 %collective-permute-start.1 = (bf16[1,128,1536]{2,1,0:T(8,128)(2,1)}, bf16[1,128,1536]{2,1,0:T(8,128)(2,1)S(1)}, u32[]{:S(2)}, u32[]{:S(2)}) collective-permute-start(bf16[1,128,1536]{2,1,0:T(8,128)(2,1)} %q.1), channel_id=1, source_target_pairs={{0,23},{1,2},{2,1},{3,4},{4,3},{5,6},{6,5},{7,8},{8,7},{9,10},{10,... | collective-permute-start | bytes 1179656 | tf_op jit(solution)/shard_map/ppermute | solution.py:330
  10.0 33.8 %collective-permute-start.9 = (bf16[128,2048]{1,0:T(8,128)(2,1)S(1)}, bf16[128,2048]{1,0:T(8,128)(2,1)S(1)}, u32[]{:S(2)}, u32[]{:S(2)}) collective-permute-start(bf16[128,2048]{1,0:T(8,128)(2,1)S(1)} %shard_map.94), channel_id=1, source_target_pairs={{0,16},{16,64},{32,48},{48,96},{64,80},{80,128},{96,112},{112,160}... | collective-permute-start | bytes 1572872 | tf_op jit(solution)/shard_map/ppermute | solution.py:327
  18.5 25.3 %collective-permute-start.10 = (bf16[128,2048]{1,0:T(8,128)(2,1)S(1)}, bf16[128,2048]{1,0:T(8,128)(2,1)S(1)}, u32[]{:S(2)}, u32[]{:S(2)}) collective-permute-start(bf16[128,2048]{1,0:T(8,128)(2,1)S(1)} %collective-permute-done.8.refs_0_), channel_id=1, source_target_pairs={{0,16},{16,0},{32,48},{48,32},{64,80},{80,64},{96,112},{112,96},{1... | collective-permute-start | bytes 1572872 | tf_op jit(solution)/shard_map/ppermute | solution.py:338
  18.5 21.1 %collective-permute-start = (bf16[1,128,1536]{2,1,0:T(8,128)(2,1)}, bf16[1,128,1536]{2,1,0:T(8,128)(2,1)S(1)}, u32[]{:S(2)}, u32[]{:S(2)}) collective-permute-start(bf16[1,128,1536]{2,1,0:T(8,128)(2,1)} %q.1), channel_id=1, source_target_pairs={{0,1},{1,0},{2,3},{3,2},{4,5},{5,4},{6,7},{7,6},{8,9},{9,8},{10,11... | collective-permute-start | bytes 1179656 | tf_op jit(solution)/shard_map/ppermute | solution.py:329
  20.4 23.3 %collective-permute-start.2 = (bf16[1,128,1536]{2,1,0:T(8,128)(2,1)S(1)}, bf16[1,128,1536]{2,1,0:T(8,128)(2,1)S(1)}, u32[]{:S(2)}, u32[]{:S(2)}) collective-permute-start(bf16[1,128,1536]{2,1,0:T(8,128)(2,1)S(1)} %collective-permute-done.1.q_two), channel_id=1, source_target_pairs={{0,16},{1,17},{2,18},{3,19},{4,20},{5,21},{6,22},{7,0},{8,15},{9,2... | collective-permute-start | bytes 1179656 | tf_op jit(solution)/shard_map/ppermute | solution.py:331
  29.6 10.1 %collective-permute-start.3 = (bf16[128,1024]{1,0:T(8,128)(2,1)S(1)}, bf16[128,1024]{1,0:T(8,128)(2,1)S(1)}, u32[]{:S(2)}, u32[]{:S(2)}) collective-permute-start(bf16[128,1024]{1,0:T(8,128)(2,1)S(1)} %shard_map.91), channel_id=1, source_target_pairs={{0,32},{16,48},{32,64},{48,80},{64,96},{80,112},{96,128},{112,144}... | collective-permute-start | bytes 786440 | tf_op jit(solution)/shard_map/ppermute | solution.py:327
  39.6 7.5 %collective-permute-start.4 = (bf16[128,1024]{1,0:T(8,128)(2,1)S(1)}, bf16[128,1024]{1,0:T(8,128)(2,1)S(1)}, u32[]{:S(2)}, u32[]{:S(2)}) collective-permute-start(bf16[128,1024]{1,0:T(8,128)(2,1)S(1)} %shard_map.91), channel_id=1, source_target_pairs={{0,16},{16,64},{32,48},{48,96},{64,80},{80,128},{96,112},{112,160}... | collective-permute-start | bytes 786440 | tf_op jit(solution)/shard_map/ppermute | solution.py:327
  39.6 7.5 %collective-permute-start.5 = (bf16[128,1024]{1,0:T(8,128)(2,1)S(1)}, bf16[128,1024]{1,0:T(8,128)(2,1)S(1)}, u32[]{:S(2)}, u32[]{:S(2)}) collective-permute-start(bf16[128,1024]{1,0:T(8,128)(2,1)S(1)} %collective-permute-done.3.refs_0_), channel_id=1, source_target_pairs={{0,16},{16,0},{32,48},{48,32},{64,80},{80,64},{96,112},{112,96},{1... | collective-permute-start | bytes 786440 | tf_op jit(solution)/shard_map/ppermute | solution.py:338
  40.3 0.7 %copy-start = (f32[4,1536]{1,0:T(4,128)S(1)}, f32[4,1536]{1,0:T(4,128)}, u32[]{:S(2)}) copy-start(f32[4,1536]{1,0:T(4,128)} %gate.1) | copy-start | bytes 73732
  41.0 0.7 %copy-start.1 = (s32[1,1,3]{2,1,0:T(1,128)S(1)}, s32[1,1,3]{2,1,0:T(1,128)}, u32[]{:S(2)}) copy-start(s32[1,1,3]{2,1,0:T(1,128)} %mask.1) | copy-start | bytes 40
  41.7 16.9 %slice-start = ((s8[4718592]{0:T(1024)(128)(4,1)}), s8[4194304]{0:T(1024)(128)(4,1)S(1)}, s32[]{:S(2)}) async-start(s8[4718592]{0:T(1024)(128)(4,1)} %bitcast), calls=%async_computation | async-start | bytes 8388608
  46.8 10.3 %collective-permute-start.11 = (bf16[136,1024]{1,0:T(8,128)(2,1)S(1)}, bf16[136,1024]{1,0:T(8,128)(2,1)S(1)}, u32[]{:S(2)}, u32[]{:S(2)}) collective-permute-start(bf16[136,1024]{1,0:T(8,128)(2,1)S(1)} %get-tuple-element.29), channel_id=1, source_target_pairs={{0,1},{1,0},{2,3},{3,2},{4,5},{5,4},{6,7},{7,6},{8,9},{9,8},{10,11... | collective-permute-start | bytes 835592 | tf_op jit(solution)/shard_map/ppermute | solution.py:341
  46.9 11.7 %slice-start.1 = ((s8[4718592]{0:T(1024)(128)(4,1)}), s8[524288]{0:T(1024)(128)(4,1)S(1)}, s32[]{:S(2)}) async-start(s8[4718592]{0:T(1024)(128)(4,1)} %bitcast), calls=%async_computation.1 | async-start | bytes 1048576
  46.9 11.7 %collective-permute-start.12 = (bf16[136,1024]{1,0:T(8,128)(2,1)S(1)}, bf16[136,1024]{1,0:T(8,128)(2,1)S(1)}, u32[]{:S(2)}, u32[]{:S(2)}) collective-permute-start(bf16[136,1024]{1,0:T(8,128)(2,1)S(1)} %get-tuple-element.30), channel_id=1, source_target_pairs={{0,16},{1,2},{2,1},{3,4},{4,3},{5,6},{6,5},{7,8},{8,7},{9,10},{10,... | collective-permute-start | bytes 835592 | tf_op jit(solution)/shard_map/ppermute | solution.py:343
  48.8 11.2 %collective-permute-start.6 = (bf16[136,512]{1,0:T(8,128)(2,1)S(1)}, bf16[136,512]{1,0:T(8,128)(2,1)S(1)}, u32[]{:S(2)}, u32[]{:S(2)}) collective-permute-start(bf16[136,512]{1,0:T(8,128)(2,1)S(1)} %get-tuple-element.23), channel_id=1, source_target_pairs={{0,1},{1,0},{2,3},{3,2},{4,5},{5,4},{6,7},{7,6},{8,9},{9,8},{10,11... | collective-permute-start | bytes 417800 | tf_op jit(solution)/shard_map/ppermute | solution.py:341
  50.6 10.5 %collective-permute-start.7 = (bf16[136,512]{1,0:T(8,128)(2,1)S(1)}, bf16[136,512]{1,0:T(8,128)(2,1)S(1)}, u32[]{:S(2)}, u32[]{:S(2)}) collective-permute-start(bf16[136,512]{1,0:T(8,128)(2,1)S(1)} %get-tuple-element.24), channel_id=1, source_target_pairs={{0,16},{1,2},{2,1},{3,4},{4,3},{5,6},{6,5},{7,8},{8,7},{9,10},{10,... | collective-permute-start | bytes 417800 | tf_op jit(solution)/shard_map/ppermute | solution.py:343
